TPU v7x, 32 devices: a whole 2x2x4 slice. The times are simulated.
32 devices in a mesh: groups: 2 (over y), tile: 16 (over z, x, core).
Axes of the slice: x: 2, y: 2, z: 4, core: 2. Of those that a mesh axis runs over, the one named last changes fastest.
Arguments:
- coarse: bfloat16 [12, 512, 512], P(None, ('groups', 'tile')), parts along dimension 1, may hold values from -6 to 6
- noise_field: bfloat16 [2, 12, 512, 512], P(None, None, ('groups', 'tile')), parts along dimension 2, may hold values from -6 to 6
- anchors: int32 [32, 2], P(('groups', 'tile')), parts along dimension 0, may hold values from 0 to 288
- counts: int32 [32], P(('groups', 'tile')), parts along dimension 0, may hold values from 1 to 2, as said below
- blend_weights: int32 [224, 224], replicated, may hold values from 1 to 16
- regress_lift: bfloat16 [12, 128], replicated, may hold values from -1.75 to 1.75
- regress_conv: bfloat16 [2, 9, 128, 128], replicated, may hold values from -0.1875 to 0.1875
- regress_head: bfloat16 [128, 12], replicated, may hold values from -0.5 to 0.5
- denoise_lift: bfloat16 [36, 128], replicated, may hold values from -1 to 1
- denoise_conv: bfloat16 [2, 9, 128, 128], replicated, may hold values from -0.1875 to 0.1875
- denoise_head: bfloat16 [128, 12], replicated, may hold values from -0.5 to 0.5
Outputs:
- ens_mean: float32 [12, 512, 512], P(None, ('groups', 'tile')), parts along dimension 1
- ens_var: float32 [12, 512, 512], P(None, ('groups', 'tile')), parts along dimension 1
There are 2 independent parts, one for each index of `groups`. A program takes and returns all parts, laid end to end along the dimension named above; an argument that names none is the same for every part. Nothing has to cross between parts.
Inputs may be any that keep to these rules, and one draw needn't show every extreme that they name: The first counts[s] slots of strip s are live; some strip has all 2 live in every draw.
All inputs are finite; a program needn't handle non-finite values.
Results may differ from a plain program's by a relative error of at most 0.0034.
Values may be sent and summed in bfloat16 or wider, within the bound.
A program may use at most 320 MiB of HBM per device.

v0:
```python
import math

import jax
import jax.numpy as jnp
from jax import lax
from jax.experimental import pallas as pl
from jax.experimental.pallas import tpu as pltpu
from jax.sharding import PartitionSpec as P

POOL = 4

skip_gain = 0.2
out_gain = 0.5 / math.sqrt(1.25)
in_gain = 1.0 / math.sqrt(1.25)


def exchange_kernel(moves, array_total, *refs):
    sources = refs[:array_total]
    targets = refs[array_total : 2 * array_total]
    send_sem, recv_sem = refs[2 * array_total :]
    mine = lax.axis_index("tile")
    count = lax.axis_size("tile")
    barrier = pltpu.get_barrier_semaphore()

    def holds(place):
        return jnp.logical_and(place >= 0, place < count)

    steps = sorted({move[3] for move in moves if move[3]})
    for step in steps:
        pl.semaphore_signal(
            barrier,
            inc=1,
            device_id={"tile": lax.rem(mine - step + count, count)},
            device_id_type=pl.DeviceIdType.MESH,
        )
    pl.semaphore_wait(barrier, len(steps))

    def copy_of(index):
        at, source, target, step = moves[index]
        return pltpu.make_async_remote_copy(
            src_ref=sources[at].at[source],
            dst_ref=targets[at].at[target],
            send_sem=send_sem.at[index],
            recv_sem=recv_sem.at[index],
            device_id={"tile": mine + step},
            device_id_type=pl.DeviceIdType.MESH,
        )

    for index, (at, source, target, step) in enumerate(moves):
        if step:

            @pl.when(holds(mine + step))
            def _():
                copy_of(index).start()

    for index, (at, source, target, step) in enumerate(moves):
        if step:

            @pl.when(jnp.logical_not(holds(mine - step)))
            def _():
                targets[at][target] = jnp.zeros(targets[at].shape[1:], targets[at].dtype)

        else:
            targets[at][target] = sources[at][source]
    for index, (at, source, target, step) in enumerate(moves):
        if step:

            @pl.when(holds(mine - step))
            def _():
                copy_of(index).wait_recv()

            @pl.when(holds(mine + step))
            def _():
                copy_of(index).wait_send()


def exchange(arrays, slots, moves, collective_id):
    vmem = pl.BlockSpec(memory_space=pltpu.VMEM)
    return pl.pallas_call(
        lambda *refs: exchange_kernel(moves, len(arrays), *refs),
        out_shape=tuple(
            jax.ShapeDtypeStruct((slot_count,) + array.shape[1:], array.dtype)
            for array, slot_count in zip(arrays, slots)
        ),
        in_specs=[vmem] * len(arrays),
        out_specs=(vmem,) * len(arrays),
        scratch_shapes=[
            pltpu.SemaphoreType.DMA((len(moves),)),
            pltpu.SemaphoreType.DMA((len(moves),)),
        ],
        compiler_params=pltpu.CompilerParams(collective_id=collective_id, has_side_effects=True),
        name="exchange%d" % collective_id,
    )(*arrays)


def conv(cells, kernel, row_pad):
    feat_in, feat_out = kernel.shape[1:]
    return lax.conv_general_dilated(
        cells,
        kernel.reshape(3, 3, feat_in, feat_out),
        (1, 1),
        ((row_pad, row_pad), (1, 1)),
        dimension_numbers=("NHWC", "HWIO", "NHWC"),
        preferred_element_type=jnp.float32,
    )


def residual_layer(hidden_act, conv_term):
    return (hidden_act.astype(jnp.float32) + jax.nn.silu(conv_term)).astype(jnp.bfloat16)


def regress(coarse, table, span, regress_lift, regress_conv, regress_head):
    channel_count, row_total, col_total = coarse.shape
    block_rows, block_cols = row_total // POOL, col_total // POOL
    layer_count = regress_conv.shape[0]
    owner = jnp.arange(col_total)[:, None] // POOL == jnp.arange(block_cols)[None, :]
    col_sums = jnp.dot(
        coarse.reshape(-1, col_total), owner.astype(jnp.bfloat16), preferred_element_type=jnp.float32
    )
    sums = col_sums.reshape(channel_count, block_rows, POOL, block_cols).sum(axis=2)
    coarse_low = (sums * (1.0 / (POOL * POOL))).astype(jnp.bfloat16)
    rows_first = coarse_low.transpose(1, 0, 2)
    rims = jnp.stack([rows_first[block_rows - layer_count :], rows_first[:layer_count]])
    moves = [(0, 0, at, at) for at in range(span - 1, -1, -1)] + [(1, 0, 0, 1), (1, 1, 1, -1)]
    tables, rims = exchange(
        (table[None], rims.reshape(2, layer_count * channel_count, block_cols)), (span, 2), moves, 0
    )
    rims = rims.reshape(2, layer_count, channel_count, block_cols)
    rimmed = jnp.concatenate([rims[0], rows_first, rims[1]]).transpose(1, 0, 2)
    hidden_act = jnp.einsum(
        "crw,ck->rwk", rimmed, regress_lift, preferred_element_type=jnp.float32
    ).astype(jnp.bfloat16)
    first_row = lax.axis_index("tile") * block_rows - layer_count
    domain_rows = lax.axis_size("tile") * block_rows
    for layer_index in range(layer_count):
        conv_term = conv(hidden_act[None], regress_conv[layer_index], 0)[0]
        hidden_act = residual_layer(hidden_act[1:-1], conv_term)
        first_row = first_row + 1
        rows = first_row + jnp.arange(hidden_act.shape[0])
        inside = jnp.logical_and(rows >= 0, rows < domain_rows)
        hidden_act = jnp.where(inside[:, None, None], hidden_act, jnp.zeros_like(hidden_act))
    reg_low = jnp.einsum(
        "rwk,kc->crw", hidden_act, regress_head, preferred_element_type=jnp.float32
    )
    wide = jnp.dot(
        reg_low.reshape(-1, block_cols),
        owner.T.astype(jnp.float32),
        precision=lax.Precision.HIGHEST,
        preferred_element_type=jnp.float32,
    ).reshape(channel_count, block_rows, 1, col_total)
    wide = jnp.broadcast_to(wide, (channel_count, block_rows, POOL, col_total))
    return coarse.astype(jnp.float32) + wide.reshape(coarse.shape), tables


def repeated(base, times):
    eye = jnp.eye(times, dtype=base.dtype)
    return (eye[:, None, :, None] * base[None, :, None, :]).reshape(
        times * base.shape[0], times * base.shape[1]
    )


def blend_kernel(slot_total, strip_rows, feat_rows, table_ref, heads_ref, weight_ref, acc_ref, den_ref):
    acc_ref[...] = jnp.zeros_like(acc_ref)
    den_ref[...] = jnp.zeros_like(den_ref)
    block_cols = heads_ref.shape[1]
    col_total = weight_ref.shape[1]

    def step(index, carry):
        offset = index // slot_total
        slot = index - offset * slot_total
        column = table_ref[offset * (slot_total + 1) + slot]
        live = slot < table_ref[offset * (slot_total + 1) + slot_total]

        @pl.when(live)
        def _():
            term = heads_ref[index]
            high = term.astype(jnp.bfloat16)
            low = (term - high.astype(jnp.float32)).astype(jnp.bfloat16)
            cols = lax.broadcasted_iota(jnp.int32, (block_cols, col_total), 1)
            blocks = lax.broadcasted_iota(jnp.int32, (block_cols, col_total), 0)
            pick = jnp.where(((cols - column) >> 2) == blocks, 1.0, 0.0).astype(jnp.bfloat16)
            dims = (((0,), (0,)), ((), ()))
            placed = lax.dot_general(
                high, pick, dims, preferred_element_type=jnp.float32
            ) + lax.dot_general(low, pick, dims, preferred_element_type=jnp.float32)
            start = pl.multiple_of(offset * strip_rows, strip_rows)
            weights = pltpu.roll(weight_ref[pl.ds(start, strip_rows), :], column, axis=1)
            den_ref[...] += weights
            for row in range(strip_rows):
                base = (row // POOL) * feat_rows
                acc_ref[row] += weights[row : row + 1, :] * placed[base : base + feat_rows, :]

        return carry

    lax.fori_loop(0, heads_ref.shape[0], step, 0)


def blend(table, heads, weights, slot_total, strip_rows, feat_rows):
    col_total = weights.shape[1]
    vmem = pl.BlockSpec(memory_space=pltpu.VMEM)
    return pl.pallas_call(
        lambda *refs: blend_kernel(slot_total, strip_rows, feat_rows, *refs),
        out_shape=(
            jax.ShapeDtypeStruct((strip_rows, feat_rows, col_total), jnp.float32),
            jax.ShapeDtypeStruct((strip_rows, col_total), jnp.float32),
        ),
        in_specs=[pl.BlockSpec(memory_space=pltpu.SMEM), vmem, vmem],
        out_specs=(vmem, vmem),
        name="blend",
    )(table, heads, weights)


def local(
    coarse,
    noise_field,
    anchors,
    counts,
    blend_weights,
    regress_lift,
    regress_conv,
    regress_head,
    denoise_lift,
    denoise_conv,
    denoise_head,
):
    members, channels, strip_rows, col_total = noise_field.shape
    patch_size = blend_weights.shape[0]
    width = denoise_lift.shape[1]
    span = patch_size // strip_rows
    slot_total = anchors.shape[1]
    block_rows = strip_rows // POOL
    block_cols = patch_size // POOL
    feat_rows = members * channels

    table = jnp.concatenate([anchors, counts[:, None]], axis=1)
    table = jnp.pad(table, ((0, 7), (0, 127 - slot_total)))
    reg_mean, tables = regress(coarse, table, span, regress_lift, regress_conv, regress_head)
    table = tables[:, 0, : slot_total + 1]

    fields = jnp.concatenate(
        [noise_field.reshape(feat_rows, strip_rows, col_total), reg_mean.astype(jnp.bfloat16), coarse]
    )
    field_count = fields.shape[0]
    row_sums = (
        fields.astype(jnp.float32)
        .reshape(field_count, block_rows, POOL, col_total)
        .sum(axis=2)
        .transpose(1, 0, 2)
    )
    row_sums = jnp.pad(row_sums, ((0, 0), (0, 0), (0, POOL - 1)))
    sums = sum(row_sums[:, :, at : at + col_total] for at in range(POOL))
    low_all = (sums * (1.0 / (POOL * POOL))).astype(jnp.bfloat16).reshape(-1, col_total)
    starts = table[:, :slot_total, None] + POOL * jnp.arange(block_cols, dtype=jnp.int32)
    pick = (starts.reshape(-1, 1) == jnp.arange(col_total, dtype=jnp.int32)[None]).astype(jnp.bfloat16)
    cut = lax.dot_general(
        pick, low_all, (((1,), (1,)), ((), ())), preferred_element_type=jnp.float32
    )
    cut = cut.astype(jnp.bfloat16).reshape(span, slot_total * block_cols, block_rows * field_count)
    farthest = range(span - 1, -1, -1)
    half = slot_total * block_cols // 2
    tail = jnp.concatenate([cut[:, :half, 128:], cut[:, half:, 128:]], axis=2)
    cut = jnp.concatenate([cut[:, :, :128], tail], axis=1)
    (low,) = exchange((cut,), (span,), [(0, at, at, -at) for at in farthest], 1)
    side = (cut.shape[2] // 2) if half else 0
    tail = low[:, 2 * half :]
    tail = jnp.concatenate([tail[:, :, :side], tail[:, :, side:]], axis=1)
    low = jnp.concatenate([low[:, : 2 * half], tail], axis=2)
    low = low.reshape(-1, block_rows * field_count)

    noise_base = repeated(denoise_lift[:channels], members)
    noise_base = jnp.pad(noise_base, ((0, 2 * channels), (0, 0)))
    cond_base = jnp.tile(denoise_lift[channels:], (1, members))
    cond_base = jnp.pad(cond_base, ((feat_rows, 0), (0, 0)))
    lifted = in_gain * jnp.dot(
        low, repeated(noise_base, block_rows), preferred_element_type=jnp.float32
    ) + jnp.dot(low, repeated(cond_base, block_rows), preferred_element_type=jnp.float32)
    hidden_act = (
        lifted.astype(jnp.bfloat16)
        .reshape(span, slot_total, block_cols, block_rows, members, width)
        .transpose(1, 4, 0, 3, 2, 5)
        .reshape(slot_total * members, span * block_rows, block_cols, width)
    )
    for layer_index in range(denoise_conv.shape[0]):
        hidden_act = residual_layer(hidden_act, conv(hidden_act, denoise_conv[layer_index], 1))
    hidden_act = (
        hidden_act.reshape(slot_total, members, span, block_rows, block_cols, width)
        .transpose(2, 0, 4, 3, 1, 5)
        .reshape(span * slot_total * block_cols, block_rows * members * width)
    )
    head = repeated(denoise_head, block_rows * members)
    head_lanes = head.shape[1]
    spare = -head_lanes % 128
    head = jnp.pad(head, ((0, 0), (0, spare)))
    heads = jnp.dot(hidden_act, head, preferred_element_type=jnp.float32)
    heads = heads.reshape(span, slot_total * block_cols, head.shape[1])
    chunks = head_lanes // spare
    lot = heads.shape[1] // (chunks + 1)
    last = heads[:, chunks * lot :]
    side = jnp.concatenate([last[:, :, at * spare : (at + 1) * spare] for at in range(chunks)], axis=1)
    heads = jnp.concatenate([heads[:, : chunks * lot, :head_lanes], side], axis=2)
    (heads,) = exchange((heads,), (span,), [(0, at, at, at) for at in farthest], 2)
    last = [heads[:, at * lot : (at + 1) * lot, head_lanes:] for at in range(chunks)]
    last = jnp.concatenate(last, axis=2)
    heads = jnp.concatenate([heads[:, :, :head_lanes], last], axis=1)
    heads = jnp.pad(heads, ((0, 0), (0, 0), (0, spare)))

    weights = jnp.pad(blend_weights.astype(jnp.float32), ((0, 0), (0, col_total - patch_size)))
    acc, denom = blend(
        table.reshape(-1),
        heads.reshape(span * slot_total, block_cols, head.shape[1]),
        weights,
        slot_total,
        strip_rows,
        feat_rows,
    )
    acc = acc.reshape(strip_rows, members, channels, col_total).transpose(1, 2, 0, 3)
    numer = skip_gain * noise_field.astype(jnp.float32) * denom + out_gain * acc
    outs = reg_mean[None] + numer / jnp.maximum(denom, 1.0)
    ens_mean = jnp.mean(outs, axis=0)
    ens_var = jnp.mean((outs - ens_mean[None]) ** 2, axis=0)
    return (ens_mean, ens_var)


def solution(mesh):
    in_specs = (
        P(None, ("groups", "tile"), None),
        P(None, None, ("groups", "tile"), None),
        P(("groups", "tile"), None),
        P(("groups", "tile")),
        P(),
        P(),
        P(),
        P(),
        P(),
        P(),
        P(),
    )
    out_specs = (P(None, ("groups", "tile"), None), P(None, ("groups", "tile"), None))
    return jax.shard_map(local, mesh=mesh, in_specs=in_specs, out_specs=out_specs, check_vma=False)
```

profile of v0, /device:TPU:25, one launch (start us, length us, event | category | flops | bytes accessed | tf_op | source)
XLA Modules:
  0.0 132.4 jit_solution(16851713748622380172)
XLA Ops:
  2.7 1.2 fusion.29
  4.6 8.1 %exchange0.1 = (s32[14,8,128]{2,1,0:T(8,128)}, bf16[2,24,128]{2,1,0:T(8,128)(2,1)}) custom-call(s32[1,8,128]{2,1,0:T(8,128)} %pad_bitcast_fusion.refs_0_, bf16[2,24,128]{2,1,0:T(8,128)(2,1)} %pad_maximum_fusion.refs_1_), custom_call_target="tpu_custom_call" | custom-call | tf_op jit(solution)/shard_map/exchange0/pallas_call | solution.py:79
  14.3 1.0 concatenate.45
  15.3 1.1 fusion.75
  21.4 1.2 convert_reduce_fusion
  26.1 15.1 %exchange1.1 = bf16[14,168,128]{2,1,0:T(8,128)(2,1)} custom-call(bf16[14,168,128]{2,1,0:T(8,128)(2,1)} %maximum_maximum_fusion.2.refs_0_), custom_call_target="tpu_custom_call" | custom-call | tf_op jit(solution)/shard_map/exchange1/pallas_call | solution.py:79
  41.2 1.2 fusion.73
  42.3 1.0 slice.119
  44.2 1.0 fusion.79
  45.2 1.0 add_convert_fusion
  46.2 3.6 %reshape.236 = bf16[14,2,56,4,2,128]{5,4,3,2,1,0:T(2,128)(2,1)} reshape(bf16[1568,1024]{1,0:T(8,128)(2,1)S(1)} %add_convert_fusion) | data formatting | bytes 6422528 | tf_op jit(solution)/shard_map/reshape | solution.py:279
  49.8 4.6 %copy.79 = bf16[2,2,14,4,56,128]{5,1,0,4,3,2:T(2,128)(2,1)S(1)} copy(bf16[2,2,14,4,56,128]{5,1,3,4,0,2:T(2,128)(2,1)} %bitcast.111) | data formatting | bytes 6422528 | tf_op jit(solution)/shard_map/transpose | solution.py:280
  54.5 11.2 %fusion.3 = bf16[4,56,56,128]{3,0,2,1:T(4,128)(2,1)S(1)} fusion(bf16[4,56,56,128]{3,0,2,1:T(4,128)(2,1)S(1)} %bitcast.117, bf16[3,3,128,128]{3,2,1,0:T(8,128)(2,1)S(1)} %bitcast.138), kind=kOutput, calls=%fused_computation.6 | convolution fusion | flops 3623059456 | bytes 6717440 | tf_op jit(solution)/shard_map/conv_general_dilated | solution.py:98
  65.7 11.4 %fusion.2 = bf16[4,56,56,128]{3,0,2,1:T(4,128)(2,1)S(1)} fusion(bf16[4,56,56,128]{3,0,2,1:T(4,128)(2,1)S(1)} %fusion.3, bf16[3,3,128,128]{3,2,1,0:T(8,128)(2,1)S(1)} %bitcast.137), kind=kOutput, calls=%fused_computation.5 | convolution fusion | flops 3623059456 | bytes 6717440 | tf_op jit(solution)/shard_map/conv_general_dilated | solution.py:98
  77.1 4.9 %copy.80 = bf16[14,2,56,4,2,128]{5,4,3,2,1,0:T(2,128)(2,1)} copy(bf16[14,2,56,4,2,128]{5,4,1,2,3,0:T(2,128)(2,1)S(1)} %bitcast.118) | data formatting | bytes 6422528 | tf_op jit(solution)/shard_map/transpose | solution.py:287
  82.0 7.0 %dot_general.39 = bf16[14,112,1024]{2,1,0:T(8,128)(2,1)S(1)} reshape(bf16[14,2,56,4,2,128]{5,4,3,2,1,0:T(2,128)(2,1)} %copy.80) | data formatting | bytes 6422528 | tf_op jit(solution)/shard_map/dot_general | solution.py:294
  89.8 1.1 copy.81
  90.9 1.0 fusion.25
  92.2 1.1 maximum_maximum_fusion.1.refs_0_
  93.3 21.2 %exchange2.1 = f32[14,84,128]{2,1,0:T(8,128)} custom-call(f32[14,84,128]{2,1,0:T(8,128)} %maximum_maximum_fusion.1.refs_0_), custom_call_target="tpu_custom_call" | custom-call | tf_op jit(solution)/shard_map/exchange2/pallas_call | solution.py:79
  114.5 1.4 %fusion.72 = (f32[14,28,32]{2,1,0:T(8,128)S(1)}, f32[14,28,32]{2,1,0:T(8,128)S(1)}, f32[14,28,32]{2,1,0:T(8,128)S(1)}) fusion(f32[14,84,128]{2,1,0:T(8,128)} %exchange2.1), kind=kLoop, calls=%fused_computation.126 | loop fusion | bytes 301056 | tf_op jit(solution)/shard_map/slice | solution.py:302
  116.0 2.2 %select_maximum_fusion = f32[14,112,128]{2,1,0:T(8,128)} fusion(f32[14,84,96]{2,1,0:T(8,128)} %bitcast.116, f32[14,28,32]{2,1,0:T(8,128)S(1)} %get-tuple-element.18, f32[14,28,32]{2,1,0:T(8,128)S(1)} %get-tuple-element.19, f32[14,28,32]{2,1,0:T(8,128)S(1)} %get-tuple-element.17), kind=kLoop, calls=%fused_computation.16 | loop fusion | flops 1605632 | bytes 1404928 | tf_op jit(solution)/shard_map/concatenate | solution.py:304
  119.0 9.6 %blend.1 = (f32[16,24,512]{2,1,0:T(8,128)}, f32[16,512]{1,0:T(8,128)}) custom-call(s32[42]{0:T(128)} %reshape_squeeze.17.refs_0_, f32[28,56,128]{2,1,0:T(8,128)} %bitcast.121, f32[224,512]{1,0:T(8,128)} %pad.34.refs_2_), custom_call_target="tpu_custom_call" | custom-call | tf_op jit(solution)/shard_map/blend/pallas_call | solution.py:201
  129.4 1.2 broadcast_multiply_fusion
  (106 shorter events, 17.1 us)
Async XLA Ops:
  0.6 16.5 %copy-start = (bf16[12,128]{1,0:T(8,128)(2,1)S(1)}, bf16[12,128]{1,0:T(8,128)(2,1)}, u32[]{:S(2)}) copy-start(bf16[12,128]{1,0:T(8,128)(2,1)} %param.16) | copy-start | bytes 9220
  0.6 17.0 %copy-start.11 = (pred[8,17]{0,1:T(8,128)(4,1)S(1)}, pred[8,17]{0,1:T(8,128)(4,1)}, u32[]{:S(2)}) copy-start(pred[8,17]{0,1:T(8,128)(4,1)} %constant.91) | copy-start | bytes 412
  18.4 1.2 copy-start.10
  18.8 1.6 %copy-start.4 = (bf16[12,16,512]{2,1,0:T(8,128)(2,1)S(1)}, bf16[12,16,512]{2,1,0:T(8,128)(2,1)}, u32[]{:S(2)}) copy-start(bf16[12,16,512]{2,1,0:T(8,128)(2,1)} %param.11) | copy-start | bytes 589828
  19.4 1.9 %copy-start.1 = (bf16[2,12,16,512]{3,2,1,0:T(8,128)(2,1)S(1)}, bf16[2,12,16,512]{3,2,1,0:T(8,128)(2,1)}, u32[]{:S(2)}) copy-start(bf16[2,12,16,512]{3,2,1,0:T(8,128)(2,1)} %param.12) | copy-start | bytes 1179652
  25.0 18.5 %copy-start.8 = (bf16[36,128]{1,0:T(8,128)(2,1)S(1)}, bf16[36,128]{1,0:T(8,128)(2,1)}, u32[]{:S(2)}) copy-start(bf16[36,128]{1,0:T(8,128)(2,1)} %param.19) | copy-start | bytes 27652
  25.0 18.6 %slice-start = ((bf16[36,128]{1,0:T(8,128)(2,1)}), bf16[12,128]{1,0:T(8,128)(2,1)S(1)}, s32[]{:S(2)}) async-start(bf16[36,128]{1,0:T(8,128)(2,1)} %param.19), calls=%async_computation | async-start | bytes 8192 | tf_op jit(solution)/shard_map/slice | solution.py:270
  49.8 4.6 %copy-start.6 = (bf16[2,9,128,128]{3,2,1,0:T(8,128)(2,1)S(1)}, bf16[2,9,128,128]{3,2,1,0:T(8,128)(2,1)}, u32[]{:S(2)}) copy-start(bf16[2,9,128,128]{3,2,1,0:T(8,128)(2,1)} %param.20) | copy-start | bytes 1769476
  82.0 7.0 %copy-start.9 = (bf16[128,12]{0,1:T(8,128)(2,1)S(1)}, bf16[128,12]{0,1:T(8,128)(2,1)}, u32[]{:S(2)}) copy-start(bf16[128,12]{0,1:T(8,128)(2,1)} %param.21) | copy-start | bytes 9220
  92.2 26.0 %copy-start.7 = (s32[224,224]{1,0:T(8,128)S(1)}, s32[224,224]{1,0:T(8,128)}, u32[]{:S(2)}) copy-start(s32[224,224]{1,0:T(8,128)} %param.15) | copy-start | bytes 602116
  118.2 12.9 %copy-start.2 = (bf16[2,12,16,512]{3,2,1,0:T(8,128)(2,1)S(1)}, bf16[2,12,16,512]{3,2,1,0:T(8,128)(2,1)}, u32[]{:S(2)}) copy-start(bf16[2,12,16,512]{3,2,1,0:T(8,128)(2,1)} %param.12) | copy-start | bytes 1179652
  118.2 13.0 %copy-start.3 = (f32[12,16,512]{2,1,0:T(8,128)S(1)}, f32[12,16,512]{2,1,0:T(8,128)}, u32[]{:S(2)}) copy-start(f32[12,16,512]{2,1,0:T(8,128)} %get-tuple-element.11) | copy-start | bytes 1179652
  131.4 1.1 copy-start.5
where the time goes:
time: 135 us; the launch traced here: 132 us
  Pallas kernels  54 us (40%)
  local copies, waits for them, and re-layouts  34.1 us (25%)
  matrix products  29.8 us (22%)
  other arithmetic  12.6 us (9%)
  between operations  1.99 us (1%)
    pallas_call x3, Pallas kernels, exchange(): pl.pallas_call(lambda *refs: exchange_kernel(moves, len(arrays), *refs),...  44.4 us
    conv_general_dilated x4, matrix products, conv(): lax.conv_general_dilated(cells, kernel.reshape(3, 3, feat_in, feat_out),...  23.8 us
    pallas_call x1, Pallas kernels, blend(): pl.pallas_call(lambda *refs: blend_kernel(slot_total, strip_rows, feat_ro...  9.63 us
    dot_general x1, local copies, waits for them, and re-layouts, local(): heads = jnp.dot(hidden_act, head, preferred_element_type=jnp.float32)  7 us
    transpose x1, local copies, waits for them, and re-layouts, local(): hidden_act = hidden_act.reshape(slot_total, members, span, block_rows, bl...  4.88 us
    transpose x1, local copies, waits for them, and re-layouts, local(): hidden_act = lifted.astype(jnp.bfloat16).reshape(span, slot_total, block_...  4.62 us
    reshape x1, local copies, waits for them, and re-layouts, local(): hidden_act = lifted.astype(jnp.bfloat16).reshape(span, slot_total, block_...  3.55 us

commit v1 on v0

v1 whole, which is shorter than its diff:
```python
import functools
import math

import jax
import jax.numpy as jnp
from jax import lax
from jax.experimental import pallas as pl
from jax.experimental.pallas import tpu as pltpu
from jax.sharding import PartitionSpec as P

POOL = 4
PAIR = 2 * POOL

skip_gain = 0.2
out_gain = 0.5 / math.sqrt(1.25)
in_gain = 1.0 / math.sqrt(1.25)

BF16 = jnp.bfloat16
F32 = jnp.float32
NN = (((1,), (0,)), ((), ()))
NT = (((1,), (1,)), ((), ()))
TN = (((0,), (0,)), ((), ()))


def mxu(lhs, rhs, dims=NN):
    return lax.dot_general(lhs, rhs, dims, preferred_element_type=F32)


def iota(shape, axis):
    return lax.broadcasted_iota(jnp.int32, shape, axis)


def one_hot(shape, rule):
    return jnp.where(rule(iota(shape, 0), iota(shape, 1)), 1.0, 0.0).astype(BF16)


def pool_rows(cells):
    cols = cells.shape[2]
    cells = cells + pltpu.roll(cells, PAIR - 1, 1)
    cells = cells + pltpu.roll(cells, PAIR - 2, 1)
    cells = cells + pltpu.roll(cells, cols - 1, 2)
    cells = cells + pltpu.roll(cells, cols - 2, 2)
    return (cells * (1.0 / (POOL * POOL))).reshape(-1, cols).astype(BF16)


def squeeze_of(channels):
    return one_hot((2 * channels, PAIR * channels), lambda r, c: c == POOL * r)


def build_taps(conv_ref, taps_ref):
    width = conv_ref.shape[2]
    for layer in range(conv_ref.shape[0]):
        for tap in range(3):
            for row_in in range(4):
                for row_out in range(2):
                    at = row_in - row_out
                    rows = pl.ds((tap * 4 + row_in) * width, width)
                    block = jnp.zeros((width, width), BF16)
                    if 0 <= at < 3:
                        block = conv_ref[layer, 3 * at + tap]
                    taps_ref[layer, rows, row_out * width : (row_out + 1) * width] = block


def shifts(cells, span):
    total, lanes = cells.shape
    column = iota((total, lanes), 0) % span
    left = jnp.where(column == 0, 0.0, pltpu.roll(cells, 1, 0))
    right = jnp.where(column == span - 1, 0.0, pltpu.roll(cells, total - 1, 0))
    return [left.astype(BF16), cells.astype(BF16), right.astype(BF16)]


def residual_pairs(parts, taps, stride):
    total, lanes = parts[0].shape
    count = total - stride
    half = lanes // 2
    lhs = jnp.concatenate([piece for part in parts for piece in (part[:count], part[stride:])], axis=1)
    term = mxu(lhs, taps)
    center = jnp.concatenate([parts[1][:count, half:], parts[1][stride:, :half]], axis=1)
    term = center.astype(F32) + term * jax.nn.sigmoid(term)
    return term.astype(BF16)


def edge_kernel(
    span,
    coarse_ref,
    noise_ref,
    table_ref,
    lift_ref,
    conv_ref,
    head_ref,
    nlow_ref,
    clow_ref,
    mean_ref,
    tables_ref,
    halo_ref,
    taps_ref,
    send_sem,
    recv_sem,
):
    channels, strip_rows, col_total = coarse_ref.shape
    width = lift_ref.shape[1]
    block_cols = col_total // POOL
    block_rows = strip_rows // POOL
    mine = lax.axis_index("tile")
    count = lax.axis_size("tile")
    barrier = pltpu.get_barrier_semaphore()

    def holds(place):
        return jnp.logical_and(place >= 0, place < count)

    moves = [
        (coarse_ref, halo_ref.at[0], 1),
        (coarse_ref, halo_ref.at[1], -1),
        (nlow_ref.at[2], nlow_ref.at[0], 1),
        (nlow_ref.at[1], nlow_ref.at[3], -1),
    ]
    moves = moves + [(table_ref.at[0], tables_ref.at[at], at) for at in range(span - 1, 0, -1)]
    steps = sorted({move[2] for move in moves})
    for step in steps:
        pl.semaphore_signal(
            barrier,
            inc=1,
            device_id={"tile": lax.rem(mine - step + count, count)},
            device_id_type=pl.DeviceIdType.MESH,
        )

    def copy_of(index):
        source, target, step = moves[index]
        return pltpu.make_async_remote_copy(
            src_ref=source,
            dst_ref=target,
            send_sem=send_sem.at[index],
            recv_sem=recv_sem.at[index],
            device_id={"tile": mine + step},
            device_id_type=pl.DeviceIdType.MESH,
        )

    def start(index):
        @pl.when(holds(mine + moves[index][2]))
        def _():
            copy_of(index).start()

    def finish(index):
        step = moves[index][2]

        @pl.when(holds(mine - step))
        def _():
            copy_of(index).wait_recv()

        @pl.when(holds(mine + step))
        def _():
            copy_of(index).wait_send()

    def clear(index):
        target, step = moves[index][1:]

        @pl.when(jnp.logical_not(holds(mine - step)))
        def _():
            target[...] = jnp.zeros(target.shape, target.dtype)

    pl.semaphore_wait(barrier, len(steps))
    for index in [0, 1] + list(range(4, len(moves))):
        start(index)
    noise = noise_ref[...].astype(F32)
    narrow = squeeze_of(2 * channels)
    for pair in range(2):
        low = pool_rows(noise[:, pair * PAIR : (pair + 1) * PAIR])
        nlow_ref[1 + pair] = mxu(narrow, low).astype(BF16)
    for index in range(len(moves)):
        clear(index)
    tables_ref[0] = table_ref[0]
    build_taps(conv_ref, taps_ref)
    start(2)
    start(3)

    pick = one_hot((block_cols, col_total), lambda r, c: c == POOL * r)
    spread = one_hot((block_cols, col_total), lambda r, c: c // POOL == r)
    by_channel = one_hot((PAIR * channels, channels), lambda r, c: r // PAIR == c)
    lift_rows = mxu(by_channel, lift_ref[...])
    at_row = iota(lift_rows.shape, 0) % PAIR
    lift_pair = jnp.concatenate(
        [jnp.where(at_row == 0, lift_rows, 0.0), jnp.where(at_row == POOL, lift_rows, 0.0)], axis=1
    ).astype(BF16)
    head_rows = mxu(by_channel, head_ref[...], NT)
    head_pair = jnp.concatenate(
        [jnp.where(at_row < POOL, head_rows, 0.0), jnp.where(at_row >= POOL, head_rows, 0.0)], axis=1
    ).astype(BF16)

    def lows_of(cells):
        cells = cells.astype(F32)
        return [pool_rows(cells[:, pair * PAIR : (pair + 1) * PAIR]) for pair in range(2)]

    def lifted(low):
        return mxu(mxu(pick, low, NT).astype(BF16), lift_pair).astype(BF16)

    own_low = lows_of(coarse_ref[...])
    own_act = [lifted(low) for low in own_low]
    finish(0)
    finish(1)
    above = halo_ref[0]
    below = halo_ref[1]
    above_low = lows_of(above)
    below_low = lows_of(below)
    acts = [lifted(low) for low in above_low] + own_act + [lifted(low) for low in below_low]
    hidden_act = jnp.concatenate(acts, axis=0).astype(F32)
    first_row = mine * block_rows - block_rows
    domain_rows = count * block_rows
    for layer in range(conv_ref.shape[0]):
        hidden_act = residual_pairs(shifts(hidden_act, block_cols), taps_ref[layer], block_cols)
        first_row = first_row + 1
        shape = hidden_act.shape
        rows = first_row + 2 * (iota(shape, 0) // block_cols) + iota(shape, 1) // width
        hidden_act = jnp.where(holds_rows(rows, domain_rows), hidden_act.astype(F32), 0.0)
    hidden_act = hidden_act.astype(BF16)

    fields = [above[:, PAIR:], coarse_ref[:, :PAIR], coarse_ref[:, PAIR:], below[:, :PAIR]]
    lows = [above_low[1]] + own_low + [below_low[0]]
    for pair in range(4):
        act = hidden_act[pair * block_cols : (pair + 1) * block_cols]
        rest = mxu(head_pair, act, NT)
        wide = 0.0
        for _ in range(3):
            part = rest.astype(BF16)
            wide = wide + mxu(part, spread)
            rest = rest - part.astype(F32)
        mean = fields[pair].astype(F32) + wide.reshape(channels, PAIR, col_total)
        if 1 <= pair <= 2:
            mean_ref[:, (pair - 1) * PAIR : pair * PAIR] = mean
        low = pool_rows(mean.astype(BF16).astype(F32))
        low = jnp.concatenate([low, lows[pair]], axis=0)
        clow_ref[pair] = mxu(narrow, low).astype(BF16)
    for index in range(2, len(moves)):
        finish(index)


def holds_rows(rows, domain_rows):
    return jnp.logical_and(rows >= 0, rows < domain_rows)


def edge(coarse, noise, table, lift, conv, head, span):
    channels, strip_rows, col_total = coarse.shape
    layers, _, width, _ = conv.shape
    vmem = pl.BlockSpec(memory_space=pltpu.VMEM)
    copies = span + 3
    return pl.pallas_call(
        functools.partial(edge_kernel, span),
        out_shape=(
            jax.ShapeDtypeStruct((4, 4 * channels, col_total), BF16),
            jax.ShapeDtypeStruct((4, 4 * channels, col_total), BF16),
            jax.ShapeDtypeStruct(coarse.shape, F32),
            jax.ShapeDtypeStruct((span, 1, 128), jnp.int32),
        ),
        in_specs=[vmem] * 6,
        out_specs=(vmem,) * 4,
        scratch_shapes=[
            pltpu.VMEM((2,) + coarse.shape, BF16),
            pltpu.VMEM((layers, 12 * width, 2 * width), BF16),
            pltpu.SemaphoreType.DMA((copies,)),
            pltpu.SemaphoreType.DMA((copies,)),
        ],
        compiler_params=pltpu.CompilerParams(collective_id=0, has_side_effects=True),
        name="edge",
    )(coarse, noise, table, lift, conv, head)


def patch_kernel(
    slot_total,
    table_ref,
    nlow_ref,
    clow_ref,
    mean_ref,
    noise_ref,
    weight_ref,
    lift_ref,
    conv_ref,
    head_ref,
    out_mean_ref,
    out_var_ref,
    taps_ref,
    field_ref,
    wide_ref,
    acc_ref,
    den_ref,
):
    feat_rows, strip_rows, col_total = noise_ref.shape
    channels = mean_ref.shape[0]
    members = feat_rows // channels
    width = lift_ref.shape[1]
    patch = weight_ref.shape[0]
    span = patch // strip_rows
    block_cols = patch // POOL
    offsets = col_total // POOL
    pad = 8

    build_taps(conv_ref, taps_ref)
    acc_ref[...] = jnp.zeros_like(acc_ref)
    den_ref[...] = jnp.zeros_like(den_ref)
    wide_ref[...] = jnp.zeros_like(wide_ref)
    wide_ref[:, :patch] = weight_ref[...].astype(F32)

    low_rows = 2 * feat_rows + 4 * channels
    noise_rows = 2 * feat_rows

    def source(row, column):
        noise_at = (row // 2) % channels
        cond_at = channels + (row - noise_rows) // 2
        return column == jnp.where(row < noise_rows, noise_at, cond_at)

    base = mxu(one_hot((low_rows, 3 * channels), source), lift_ref[...])
    row = iota(base.shape, 0)
    blocks = []
    for member in range(members):
        first = 2 * channels * member
        for half in range(2):
            keep = (row >= first) & (row < first + 2 * channels) & (row % 2 == half)
            blocks.append(jnp.where(keep, base, 0.0))
    noise_lift = jnp.concatenate(blocks, axis=1).astype(BF16)
    cond_lift = jnp.concatenate(
        [jnp.where((row >= noise_rows) & (row % 2 == half), base, 0.0) for half in range(2)], axis=1
    ).astype(BF16)
    order = one_hot((col_total, col_total), lambda r, c: c == POOL * (r % offsets) + r // offsets)
    for pair in range(4):
        low = jnp.concatenate([nlow_ref[pair], clow_ref[pair]], axis=0)
        turned = mxu(order, low, NT).astype(BF16)
        cond = mxu(turned, cond_lift)
        act = in_gain * mxu(turned, noise_lift) + jnp.concatenate([cond] * members, axis=1)
        act = act.astype(BF16).astype(F32)
        for phase in range(POOL):
            for member in range(members):
                for half in range(2):
                    first = (member * 2 + half) * width
                    field_ref[phase, pair * members + member, half, pad : pad + offsets] = act[
                        phase * offsets : (phase + 1) * offsets, first : first + width
                    ]

    lanes = 128
    head_wide = one_hot((channels, lanes), lambda r, c: (c % channels == r) & (c < 4 * feat_rows))
    head_wide = mxu(head_ref[...], head_wide)
    lane = iota(head_wide.shape, 1)
    heads = []
    for pair in range(2):
        for member in range(members):
            for half in range(2):
                first = (2 * pair + half) * feat_rows + member * channels
                keep = (lane >= first) & (lane < first + channels)
                heads.append(jnp.where(keep, head_wide, 0.0))
    heads = jnp.concatenate(heads, axis=0).astype(BF16)

    stride = members * block_cols

    def step(index, carry):
        offset = index // slot_total
        slot = index - offset * slot_total
        column = table_ref[offset, 0, slot]
        live = slot < table_ref[offset, 0, slot_total]

        @pl.when(live)
        def _():
            phase = column & (POOL - 1)
            start = (column >> 2) + pad
            is_top = offset == 0
            is_bottom = offset == span - 1
            cell = iota((block_cols, 2 * width), 0)
            parts = []
            for tap in range(3):
                rows = []
                for pair in range(4):
                    for member in range(members):
                        which = pair * members + member
                        window = pl.ds(start + tap - 1, block_cols)
                        at = jnp.concatenate([field_ref[phase, which, half, window, :] for half in range(2)], axis=1)
                        if tap == 0:
                            at = jnp.where(cell == 0, 0.0, at)
                        if tap == 2:
                            at = jnp.where(cell == block_cols - 1, 0.0, at)
                        if pair == 0:
                            at = jnp.where(is_top, 0.0, at)
                        if pair == 3:
                            at = jnp.where(is_bottom, 0.0, at)
                        rows.append(at)
                parts.append(jnp.concatenate(rows, axis=0).astype(BF16))
            act = residual_pairs(parts, taps_ref[0], stride).astype(F32)
            side = iota((stride, 2 * width), 1) // width
            top = jnp.where(jnp.logical_and(is_top, side == 0), 0.0, act[:stride])
            bottom = jnp.where(jnp.logical_and(is_bottom, side == 1), 0.0, act[2 * stride :])
            act = jnp.concatenate([top, act[stride : 2 * stride], bottom], axis=0)
            act = residual_pairs(shifts(act, block_cols), taps_ref[1], stride).astype(F32)
            act = jnp.concatenate(
                [act[at * block_cols : (at + 1) * block_cols] for at in range(2 * members)], axis=1
            ).astype(BF16)
            term = mxu(act, heads)
            high = term.astype(BF16)
            low = (term - high.astype(F32)).astype(BF16)
            cols = iota((block_cols, col_total), 1)
            blocks = iota((block_cols, col_total), 0)
            place = jnp.where(((cols - column) >> 2) == blocks, 1.0, 0.0).astype(BF16)
            placed = mxu(high, place, TN) + mxu(low, place, TN)
            first = pl.multiple_of(offset * strip_rows, strip_rows)
            weights = pltpu.roll(wide_ref[pl.ds(first, strip_rows), :], column, axis=1)
            den_ref[...] += weights
            for at in range(strip_rows):
                below = (at // POOL) * feat_rows
                acc_ref[at] += weights[at : at + 1, :] * placed[below : below + feat_rows, :]

        return carry

    lax.fori_loop(0, span * slot_total, step, 0)

    denom = den_ref[...]
    scale = 1.0 / jnp.maximum(denom, 1.0)
    for channel in range(channels):
        outs = []
        for member in range(members):
            at = member * channels + channel
            numer = skip_gain * noise_ref[at].astype(F32) * denom + out_gain * acc_ref[:, at, :]
            outs.append(mean_ref[channel] + numer * scale)
        ens_mean = sum(outs) * (1.0 / members)
        out_mean_ref[channel] = ens_mean
        out_var_ref[channel] = sum((out - ens_mean) ** 2 for out in outs) * (1.0 / members)


def patches(tables, nlow, clow, mean, noise, weights, lift, conv, head, slot_total):
    feat_rows, strip_rows, col_total = noise.shape
    layers, _, width, _ = conv.shape
    members = feat_rows // mean.shape[0]
    vmem = pl.BlockSpec(memory_space=pltpu.VMEM)
    return pl.pallas_call(
        functools.partial(patch_kernel, slot_total),
        out_shape=(jax.ShapeDtypeStruct(mean.shape, F32),) * 2,
        in_specs=[pl.BlockSpec(memory_space=pltpu.SMEM)] + [vmem] * 8,
        out_specs=(vmem, vmem),
        scratch_shapes=[
            pltpu.VMEM((layers, 12 * width, 2 * width), BF16),
            pltpu.VMEM((POOL, 4 * members, 2, col_total // POOL + 16, width), F32),
            pltpu.VMEM((weights.shape[0], col_total), F32),
            pltpu.VMEM((strip_rows, feat_rows, col_total), F32),
            pltpu.VMEM((strip_rows, col_total), F32),
        ],
        name="patches",
    )(tables, nlow, clow, mean, noise, weights, lift, conv, head)


def local(
    coarse,
    noise_field,
    anchors,
    counts,
    blend_weights,
    regress_lift,
    regress_conv,
    regress_head,
    denoise_lift,
    denoise_conv,
    denoise_head,
):
    members, channels, strip_rows, col_total = noise_field.shape
    span = blend_weights.shape[0] // strip_rows
    slot_total = anchors.shape[1]
    noise = noise_field.reshape(members * channels, strip_rows, col_total)
    table = jnp.concatenate([anchors, counts[:, None]], axis=1)
    table = jnp.pad(table, ((0, 0), (0, 127 - slot_total)))[None]
    nlow, clow, mean, tables = edge(coarse, noise, table, regress_lift, regress_conv, regress_head, span)
    return patches(
        tables, nlow, clow, mean, noise, blend_weights, denoise_lift, denoise_conv, denoise_head, slot_total
    )


def solution(mesh):
    in_specs = (
        P(None, ("groups", "tile"), None),
        P(None, None, ("groups", "tile"), None),
        P(("groups", "tile"), None),
        P(("groups", "tile")),
        P(),
        P(),
        P(),
        P(),
        P(),
        P(),
        P(),
    )
    out_specs = (P(None, ("groups", "tile"), None), P(None, ("groups", "tile"), None))
    return jax.shard_map(local, mesh=mesh, in_specs=in_specs, out_specs=out_specs, check_vma=False)
```

time: 135 us -> 64.3 us (0.48)
  the two profiles are of different devices: /device:TPU:25 before, /device:TPU:29 now
where the time goes in v1:
time: 64.3 us; the launch traced here: 64.9 us
  Pallas kernels  61.5 us (96%)
  local copies, waits for them, and re-layouts  2.05 us (3%)
  between operations  1.32 us (2%)
    pallas_call x1, Pallas kernels, patches(): pl.pallas_call(functools.partial(patch_kernel, slot_total), out_shape=(ja...  45 us
    pallas_call x1, Pallas kernels, edge(): pl.pallas_call(functools.partial(edge_kernel, span), out_shape=(jax.Shape...  16.5 us
    unnamed x8, local copies, waits for them, and re-layouts  1.53 us

profile of v1, /device:TPU:29, one launch (start us, length us, event | category | flops | bytes accessed | tf_op | source)
XLA Modules:
  0.0 64.9 jit_solution(9496427100732277078)
XLA Ops:
  0.6 0.0 copy-start.2
  1.3 0.0 copy-start
  1.3 0.0 copy-done.2
  1.3 0.1 pad_add_fusion
  1.4 0.5 pad_bitcast_fusion.table_ref
  1.9 0.1 copy-done
  2.0 0.0 copy-start.1
  2.0 0.7 %copy.13.head_ref = bf16[128,12]{1,0:T(8,128)(2,1)} copy(bf16[128,12]{0,1:T(8,128)(2,1)S(1)} %copy-done) | data formatting | bytes 6144 | tf_op args[7]
  2.7 0.0 copy-done.1
  2.7 0.7 %copy.14.head_ref = bf16[128,12]{1,0:T(8,128)(2,1)} copy(bf16[128,12]{0,1:T(8,128)(2,1)S(1)} %copy-done.1) | data formatting | bytes 6144 | tf_op args[10]
  3.4 16.5 %edge.1 = (bf16[4,48,512]{2,1,0:T(8,128)(2,1)}, bf16[4,48,512]{2,1,0:T(8,128)(2,1)}, f32[12,16,512]{2,1,0:T(8,128)}, s32[14,1,128]{2,1,0:T(1,128)}) custom-call(bf16[12,16,512]{2,1,0:T(8,128)(2,1)} %coarse_ref.1, bf16[24,16,512]{2,1,0:T(8,128)(2,1)} %bitcast.5, s32[1,1,128]{2,1,0:T(1,128)} %pad_bitcast_fusion.table_ref, bf16[12,128]{1,0:T(8,128)(2,1)} %lift_ref.2, ...), custom_call_target="tpu_custom_call" | custom-call | tf_op jit(solution)/shard_map/edge/pallas_call | solution.py:245
  19.9 45.0 %patches.1 = (f32[12,16,512]{2,1,0:T(8,128)}, f32[12,16,512]{2,1,0:T(8,128)}) custom-call(s32[14,1,128]{2,1,0:T(1,128)} %get-tuple-element.6.table_ref, bf16[4,48,512]{2,1,0:T(8,128)(2,1)} %get-tuple-element.7.nlow_ref, bf16[4,48,512]{2,1,0:T(8,128)(2,1)} %get-tuple-element.8.clow_ref, f32[12,16,512]{2,1,0:T(8,128)} %get-tuple-element.9.mean_ref, ...), custom_call_target="tpu_custom_call" | custom-call | tf_op jit(solution)/shard_map/patches/pallas_call | solution.py:427
Async XLA Ops:
  0.6 0.7 %copy-start.2 = (s32[1,2]{1,0:T(1,128)S(1)}, s32[1,2]{1,0:T(1,128)}, u32[]{:S(2)}) copy-start(s32[1,2]{1,0:T(1,128)} %param.13) | copy-start | bytes 28
  1.3 0.7 %copy-start = (bf16[128,12]{0,1:T(8,128)(2,1)S(1)}, bf16[128,12]{0,1:T(8,128)(2,1)}, u32[]{:S(2)}) copy-start(bf16[128,12]{0,1:T(8,128)(2,1)} %param.18) | copy-start | bytes 9220
  2.0 0.7 %copy-start.1 = (bf16[128,12]{0,1:T(8,128)(2,1)S(1)}, bf16[128,12]{0,1:T(8,128)(2,1)}, u32[]{:S(2)}) copy-start(bf16[128,12]{0,1:T(8,128)(2,1)} %param.21) | copy-start | bytes 9220

commit v2 on v1

--- a/solution.py
+++ b/solution.py
@@ -10,6 +10,7 @@
 
 POOL = 4
 PAIR = 2 * POOL
+GROUP = 2
 
 skip_gain = 0.2
 out_gain = 0.5 / math.sqrt(1.25)
@@ -281,6 +282,8 @@
     wide_ref,
     acc_ref,
     den_ref,
+    stage_ref,
+    list_ref,
 ):
     feat_rows, strip_rows, col_total = noise_ref.shape
     channels = mean_ref.shape[0]
@@ -346,65 +349,115 @@
                 heads.append(jnp.where(keep, head_wide, 0.0))
     heads = jnp.concatenate(heads, axis=0).astype(BF16)
 
-    stride = members * block_cols
-
-    def step(index, carry):
+    group = stage_ref.shape[1]
+    slots = 4 * members
+    stage_ref[...] = jnp.zeros_like(stage_ref)
+    field_ref[:, slots] = jnp.zeros(field_ref.shape[:1] + field_ref.shape[2:], F32)
+    stride = group * members * block_cols
+    reach = 3 * lanes
+
+    def note(index, found):
         offset = index // slot_total
         slot = index - offset * slot_total
-        column = table_ref[offset, 0, slot]
         live = slot < table_ref[offset, 0, slot_total]
 
         @pl.when(live)
         def _():
-            phase = column & (POOL - 1)
-            start = (column >> 2) + pad
-            is_top = offset == 0
-            is_bottom = offset == span - 1
-            cell = iota((block_cols, 2 * width), 0)
-            parts = []
-            for tap in range(3):
+            list_ref[found] = index
+
+        return found + live.astype(jnp.int32)
+
+    def blank(index, carry):
+        list_ref[index] = 0
+        return carry
+
+    lax.fori_loop(0, list_ref.shape[0], blank, 0)
+    live_total = lax.fori_loop(0, span * slot_total, note, 0)
+
+    def step(turn, carry):
+        pieces = []
+        for at in range(group):
+            place = turn * group + at
+            index = list_ref[place]
+            offset = index // slot_total
+            column = table_ref[offset, 0, index - offset * slot_total]
+            pieces.append((offset, column, place < live_total))
+        edge_cell = iota((8, width), 0)
+        parts = []
+        for tap in range(3):
+            sides = []
+            for half in range(2):
                 rows = []
                 for pair in range(4):
+                    for offset, column, _ in pieces:
+                        phase = column & (POOL - 1)
+                        window = pl.ds((column >> 2) + pad + tap - 1, block_cols)
+                        for member in range(members):
+                            which = pair * members + member
+                            if pair == 0:
+                                which = jnp.where(offset == 0, slots, which)
+                            if pair == 3:
+                                which = jnp.where(offset == span - 1, slots, which)
+                            at = field_ref[phase, which, half, window, :]
+                            if tap == 0:
+                                at = jnp.concatenate([jnp.where(edge_cell == 0, 0.0, at[:8]), at[8:]], axis=0)
+                            if tap == 2:
+                                at = jnp.concatenate([at[:-8], jnp.where(edge_cell == 7, 0.0, at[-8:])], axis=0)
+                            rows.append(at)
+                sides.append(jnp.concatenate(rows, axis=0))
+            parts.append(jnp.concatenate(sides, axis=1).astype(BF16))
+        act = residual_pairs(parts, taps_ref[0], stride).astype(F32)
+        parts = [[], [], []]
+        for half in range(2):
+            rows = [[], [], []]
+            for pair in range(3):
+                for at, (offset, _, _) in enumerate(pieces):
                     for member in range(members):
-                        which = pair * members + member
-                        window = pl.ds(start + tap - 1, block_cols)
-                        at = jnp.concatenate([field_ref[phase, which, half, window, :] for half in range(2)], axis=1)
-                        if tap == 0:
-                            at = jnp.where(cell == 0, 0.0, at)
-                        if tap == 2:
-                            at = jnp.where(cell == block_cols - 1, 0.0, at)
-                        if pair == 0:
-                            at = jnp.where(is_top, 0.0, at)
-                        if pair == 3:
-                            at = jnp.where(is_bottom, 0.0, at)
-                        rows.append(at)
-                parts.append(jnp.concatenate(rows, axis=0).astype(BF16))
-            act = residual_pairs(parts, taps_ref[0], stride).astype(F32)
-            side = iota((stride, 2 * width), 1) // width
-            top = jnp.where(jnp.logical_and(is_top, side == 0), 0.0, act[:stride])
-            bottom = jnp.where(jnp.logical_and(is_bottom, side == 1), 0.0, act[2 * stride :])
-            act = jnp.concatenate([top, act[stride : 2 * stride], bottom], axis=0)
-            act = residual_pairs(shifts(act, block_cols), taps_ref[1], stride).astype(F32)
-            act = jnp.concatenate(
-                [act[at * block_cols : (at + 1) * block_cols] for at in range(2 * members)], axis=1
-            ).astype(BF16)
-            term = mxu(act, heads)
+                        first = ((pair * group + at) * members + member) * block_cols
+                        cells = act[first : first + block_cols, half * width : (half + 1) * width]
+                        if pair == 0 and half == 0:
+                            cells = jnp.where(offset == 0, 0.0, cells)
+                        if pair == 2 and half == 1:
+                            cells = jnp.where(offset == span - 1, 0.0, cells)
+                        hold = stage_ref.at[half, at, pair * members + member]
+                        hold[8 : 8 + block_cols] = cells
+                        rows[0].append(hold[7 : 7 + block_cols])
+                        rows[1].append(cells)
+                        rows[2].append(hold[9 : 9 + block_cols])
+            for tap in range(3):
+                parts[tap].append(jnp.concatenate(rows[tap], axis=0))
+        parts = [jnp.concatenate(sides, axis=1).astype(BF16) for sides in parts]
+        act = residual_pairs(parts, taps_ref[1], stride).astype(F32)
+        rows = []
+        for at in range(group):
+            sides = []
+            for pair in range(2):
+                for member in range(members):
+                    first = ((pair * group + at) * members + member) * block_cols
+                    sides.append(act[first : first + block_cols])
+            rows.append(jnp.concatenate(sides, axis=1))
+        terms = mxu(jnp.concatenate(rows, axis=0).astype(BF16), heads)
+        cols = iota((block_cols, reach), 1)
+        blocks = iota((block_cols, reach), 0)
+        for at, (offset, column, live) in enumerate(pieces):
+            term = terms[at * block_cols : (at + 1) * block_cols]
             high = term.astype(BF16)
             low = (term - high.astype(F32)).astype(BF16)
-            cols = iota((block_cols, col_total), 1)
-            blocks = iota((block_cols, col_total), 0)
-            place = jnp.where(((cols - column) >> 2) == blocks, 1.0, 0.0).astype(BF16)
+            first = jnp.minimum(column // lanes, col_total // lanes - 3) * lanes
+            inner = column - first
+            span_cols = pl.ds(pl.multiple_of(first, lanes), reach)
+            place = jnp.where(((cols - inner) >> 2) == blocks, 1.0, 0.0).astype(BF16)
             placed = mxu(high, place, TN) + mxu(low, place, TN)
-            first = pl.multiple_of(offset * strip_rows, strip_rows)
-            weights = pltpu.roll(wide_ref[pl.ds(first, strip_rows), :], column, axis=1)
-            den_ref[...] += weights
-            for at in range(strip_rows):
-                below = (at // POOL) * feat_rows
-                acc_ref[at] += weights[at : at + 1, :] * placed[below : below + feat_rows, :]
-
+            top = pl.multiple_of(offset * strip_rows, strip_rows)
+            weights = pltpu.roll(wide_ref[pl.ds(top, strip_rows), :], inner, axis=1)
+            weights = jnp.where(live, weights, 0.0)
+            den_ref[:, span_cols] += weights
+            for row in range(strip_rows):
+                below = (row // POOL) * feat_rows
+                acc_ref[row, :, span_cols] += weights[row : row + 1, :] * placed[below : below + feat_rows, :]
         return carry
 
-    lax.fori_loop(0, span * slot_total, step, 0)
+    lax.fori_loop(0, (live_total + group - 1) // group, step, 0)
 
     denom = den_ref[...]
     scale = 1.0 / jnp.maximum(denom, 1.0)
@@ -431,10 +484,12 @@
         out_specs=(vmem, vmem),
         scratch_shapes=[
             pltpu.VMEM((layers, 12 * width, 2 * width), BF16),
-            pltpu.VMEM((POOL, 4 * members, 2, col_total // POOL + 16, width), F32),
-            pltpu.VMEM((weights.shape[0], col_total), F32),
+            pltpu.VMEM((POOL, 4 * members + 1, 2, col_total // POOL + 16, width), F32),
+            pltpu.VMEM((weights.shape[0], 3 * 128), F32),
             pltpu.VMEM((strip_rows, feat_rows, col_total), F32),
             pltpu.VMEM((strip_rows, col_total), F32),
+            pltpu.VMEM((2, GROUP, 3 * members, weights.shape[0] // POOL + 16, width), F32),
+            pltpu.SMEM((weights.shape[0] // strip_rows * slot_total + GROUP,), jnp.int32),
         ],
         name="patches",
     )(tables, nlow, clow, mean, noise, weights, lift, conv, head)

time: 64.3 us -> 58.3 us (0.907)
  the two profiles are of different devices: /device:TPU:29 before, /device:TPU:25 now
where the time goes in v2:
time: 58.3 us; the launch traced here: 57.8 us
  Pallas kernels  54.4 us (93%)
  local copies, waits for them, and re-layouts  2.05 us (4%)
  between operations  1.32 us (2%)
    pallas_call x1, Pallas kernels, patches(): pl.pallas_call(functools.partial(patch_kernel, slot_total), out_shape=(ja...  37.9 us
    pallas_call x1, Pallas kernels, edge(): pl.pallas_call(functools.partial(edge_kernel, span), out_shape=(jax.Shape...  16.5 us
    unnamed x8, local copies, waits for them, and re-layouts  1.53 us

profile of v2, /device:TPU:25, one launch (start us, length us, event | category | flops | bytes accessed | tf_op | source)
XLA Modules:
  0.0 57.8 jit_solution(6291569117414998821)
XLA Ops:
  0.6 0.0 copy-start.2
  1.3 0.0 copy-start
  1.3 0.0 copy-done.2
  1.3 0.1 pad_add_fusion
  1.4 0.5 pad_bitcast_fusion.table_ref
  1.9 0.1 copy-done
  2.0 0.0 copy-start.1
  2.0 0.7 %copy.13.head_ref = bf16[128,12]{1,0:T(8,128)(2,1)} copy(bf16[128,12]{0,1:T(8,128)(2,1)S(1)} %copy-done) | data formatting | bytes 6144 | tf_op args[7]
  2.7 0.0 copy-done.1
  2.7 0.7 %copy.14.head_ref = bf16[128,12]{1,0:T(8,128)(2,1)} copy(bf16[128,12]{0,1:T(8,128)(2,1)S(1)} %copy-done.1) | data formatting | bytes 6144 | tf_op args[10]
  3.4 16.5 %edge.1 = (bf16[4,48,512]{2,1,0:T(8,128)(2,1)}, bf16[4,48,512]{2,1,0:T(8,128)(2,1)}, f32[12,16,512]{2,1,0:T(8,128)}, s32[14,1,128]{2,1,0:T(1,128)}) custom-call(bf16[12,16,512]{2,1,0:T(8,128)(2,1)} %coarse_ref.1, bf16[24,16,512]{2,1,0:T(8,128)(2,1)} %bitcast.5, s32[1,1,128]{2,1,0:T(1,128)} %pad_bitcast_fusion.table_ref, bf16[12,128]{1,0:T(8,128)(2,1)} %lift_ref.2, ...), custom_call_target="tpu_custom_call" | custom-call | tf_op jit(solution)/shard_map/edge/pallas_call | solution.py:246
  19.9 37.9 %patches.1 = (f32[12,16,512]{2,1,0:T(8,128)}, f32[12,16,512]{2,1,0:T(8,128)}) custom-call(s32[14,1,128]{2,1,0:T(1,128)} %get-tuple-element.6.table_ref, bf16[4,48,512]{2,1,0:T(8,128)(2,1)} %get-tuple-element.7.nlow_ref, bf16[4,48,512]{2,1,0:T(8,128)(2,1)} %get-tuple-element.8.clow_ref, f32[12,16,512]{2,1,0:T(8,128)} %get-tuple-element.9.mean_ref, ...), custom_call_target="tpu_custom_call" | custom-call | tf_op jit(solution)/shard_map/patches/pallas_call | solution.py:480
Async XLA Ops:
  0.6 0.7 %copy-start.2 = (s32[1,2]{1,0:T(1,128)S(1)}, s32[1,2]{1,0:T(1,128)}, u32[]{:S(2)}) copy-start(s32[1,2]{1,0:T(1,128)} %param.13) | copy-start | bytes 28
  1.3 0.7 %copy-start = (bf16[128,12]{0,1:T(8,128)(2,1)S(1)}, bf16[128,12]{0,1:T(8,128)(2,1)}, u32[]{:S(2)}) copy-start(bf16[128,12]{0,1:T(8,128)(2,1)} %param.18) | copy-start | bytes 9220
  2.0 0.7 %copy-start.1 = (bf16[128,12]{0,1:T(8,128)(2,1)S(1)}, bf16[128,12]{0,1:T(8,128)(2,1)}, u32[]{:S(2)}) copy-start(bf16[128,12]{0,1:T(8,128)(2,1)} %param.21) | copy-start | bytes 9220

commit v3 on v2

--- a/solution.py
+++ b/solution.py
@@ -10,7 +10,7 @@
 
 POOL = 4
 PAIR = 2 * POOL
-GROUP = 2
+GROUP = 3
 
 skip_gain = 0.2
 out_gain = 0.5 / math.sqrt(1.25)
@@ -35,17 +35,24 @@
     return jnp.where(rule(iota(shape, 0), iota(shape, 1)), 1.0, 0.0).astype(BF16)
 
 
-def pool_rows(cells):
-    cols = cells.shape[2]
-    cells = cells + pltpu.roll(cells, PAIR - 1, 1)
-    cells = cells + pltpu.roll(cells, PAIR - 2, 1)
-    cells = cells + pltpu.roll(cells, cols - 1, 2)
-    cells = cells + pltpu.roll(cells, cols - 2, 2)
-    return (cells * (1.0 / (POOL * POOL))).reshape(-1, cols).astype(BF16)
-
-
-def squeeze_of(channels):
-    return one_hot((2 * channels, PAIR * channels), lambda r, c: c == POOL * r)
+def pool_of(pairs, channels):
+    depth = PAIR * pairs
+
+    def rule(row, column):
+        pair = row // (2 * channels)
+        channel = row % (2 * channels) // 2
+        block = 2 * pair + row % 2
+        return (channel == column // depth) & (block == column % depth // POOL)
+
+    return one_hot((2 * pairs * channels, depth * channels), rule)
+
+
+def pooled(rule, cells):
+    cols = cells.shape[-1]
+    sums = mxu(rule, cells.reshape(-1, cols))
+    sums = sums + pltpu.roll(sums, cols - 1, 1)
+    sums = sums + pltpu.roll(sums, cols - 2, 1)
+    return sums * (1.0 / (POOL * POOL))
 
 
 def build_taps(conv_ref, taps_ref):
@@ -59,23 +66,35 @@
                     block = jnp.zeros((width, width), BF16)
                     if 0 <= at < 3:
                         block = conv_ref[layer, 3 * at + tap]
+                    if tap * 4 + row_in >= 6:
+                        block = -block
                     taps_ref[layer, rows, row_out * width : (row_out + 1) * width] = block
 
 
-def shifts(cells, span):
-    total, lanes = cells.shape
-    column = iota((total, lanes), 0) % span
-    left = jnp.where(column == 0, 0.0, pltpu.roll(cells, 1, 0))
-    right = jnp.where(column == span - 1, 0.0, pltpu.roll(cells, total - 1, 0))
-    return [left.astype(BF16), cells.astype(BF16), right.astype(BF16)]
+def shifts(cells, holds):
+    parts = [[], [], []]
+    for half, runs in enumerate(cells):
+        rows = [[], [], []]
+        for at, run in enumerate(runs):
+            count = run.shape[0]
+            hold = holds(half, at)
+            hold[8 : 8 + count] = run
+            rows[0].append(hold[7 : 7 + count])
+            rows[1].append(run)
+            rows[2].append(hold[9 : 9 + count])
+        for tap in range(3):
+            parts[tap].append(jnp.concatenate(rows[tap], axis=0))
+    return [jnp.concatenate(sides, axis=1).astype(BF16) for sides in parts]
 
 
 def residual_pairs(parts, taps, stride):
     total, lanes = parts[0].shape
     count = total - stride
     half = lanes // 2
-    lhs = jnp.concatenate([piece for part in parts for piece in (part[:count], part[stride:])], axis=1)
-    term = mxu(lhs, taps)
+    pieces = [piece for part in parts for piece in (part[:count], part[stride:])]
+    depth = taps.shape[0] // 2
+    term = mxu(jnp.concatenate(pieces[:3], axis=1), taps[:depth])
+    term = term - mxu(jnp.concatenate(pieces[3:], axis=1), taps[depth:])
     center = jnp.concatenate([parts[1][:count, half:], parts[1][stride:, :half]], axis=1)
     term = center.astype(F32) + term * jax.nn.sigmoid(term)
     return term.astype(BF16)
@@ -95,6 +114,7 @@
     tables_ref,
     halo_ref,
     taps_ref,
+    stage_ref,
     send_sem,
     recv_sem,
 ):
@@ -162,11 +182,9 @@
     pl.semaphore_wait(barrier, len(steps))
     for index in [0, 1] + list(range(4, len(moves))):
         start(index)
-    noise = noise_ref[...].astype(F32)
-    narrow = squeeze_of(2 * channels)
+    low = pooled(pool_of(2, 2 * channels), noise_ref[...]).astype(BF16)
     for pair in range(2):
-        low = pool_rows(noise[:, pair * PAIR : (pair + 1) * PAIR])
-        nlow_ref[1 + pair] = mxu(narrow, low).astype(BF16)
+        nlow_ref[1 + pair] = low[pair * 4 * channels : (pair + 1) * 4 * channels]
     for index in range(len(moves)):
         clear(index)
     tables_ref[0] = table_ref[0]
@@ -176,66 +194,74 @@
 
     pick = one_hot((block_cols, col_total), lambda r, c: c == POOL * r)
     spread = one_hot((block_cols, col_total), lambda r, c: c // POOL == r)
-    by_channel = one_hot((PAIR * channels, channels), lambda r, c: r // PAIR == c)
-    lift_rows = mxu(by_channel, lift_ref[...])
-    at_row = iota(lift_rows.shape, 0) % PAIR
-    lift_pair = jnp.concatenate(
-        [jnp.where(at_row == 0, lift_rows, 0.0), jnp.where(at_row == POOL, lift_rows, 0.0)], axis=1
-    ).astype(BF16)
-    head_rows = mxu(by_channel, head_ref[...], NT)
-    head_pair = jnp.concatenate(
-        [jnp.where(at_row < POOL, head_rows, 0.0), jnp.where(at_row >= POOL, head_rows, 0.0)], axis=1
-    ).astype(BF16)
+    lift_rows = mxu(one_hot((2 * channels, channels), lambda r, c: r // 2 == c), lift_ref[...])
+    at_row = iota(lift_rows.shape, 0) % 2
+    lift_pair = jnp.concatenate([jnp.where(at_row == half, lift_rows, 0.0) for half in range(2)], axis=1)
+    lift_pair = lift_pair.astype(BF16)
+    head_rows = mxu(one_hot((PAIR * channels, channels), lambda r, c: r // PAIR == c), head_ref[...])
+    at_row = iota(head_rows.shape, 0) % PAIR // POOL
+    head_pair = jnp.concatenate([jnp.where(at_row == half, head_rows, 0.0) for half in range(2)], axis=1)
+    head_pair = head_pair.astype(BF16)
+    stage_ref[:, :, :8] = jnp.zeros(stage_ref.shape[:2] + (8, width), F32)
+    stage_ref[:, :, 8 + block_cols :] = jnp.zeros(stage_ref.shape[:2] + (8, width), F32)
+
+    strip_rule = pool_of(2, channels)
+    pair_rule = pool_of(1, channels)
+    low_rows = 2 * channels
 
     def lows_of(cells):
-        cells = cells.astype(F32)
-        return [pool_rows(cells[:, pair * PAIR : (pair + 1) * PAIR]) for pair in range(2)]
+        low = pooled(strip_rule, cells)
+        return [low[:low_rows], low[low_rows:]]
 
     def lifted(low):
-        return mxu(mxu(pick, low, NT).astype(BF16), lift_pair).astype(BF16)
+        act = mxu(mxu(pick, low.astype(BF16), NT).astype(BF16), lift_pair)
+        return act.astype(BF16).astype(F32)
 
     own_low = lows_of(coarse_ref[...])
     own_act = [lifted(low) for low in own_low]
     finish(0)
     finish(1)
-    above = halo_ref[0]
-    below = halo_ref[1]
-    above_low = lows_of(above)
-    below_low = lows_of(below)
+    above_low = lows_of(halo_ref[0])
+    below_low = lows_of(halo_ref[1])
     acts = [lifted(low) for low in above_low] + own_act + [lifted(low) for low in below_low]
-    hidden_act = jnp.concatenate(acts, axis=0).astype(F32)
-    first_row = mine * block_rows - block_rows
     domain_rows = count * block_rows
-    for layer in range(conv_ref.shape[0]):
-        hidden_act = residual_pairs(shifts(hidden_act, block_cols), taps_ref[layer], block_cols)
-        first_row = first_row + 1
-        shape = hidden_act.shape
-        rows = first_row + 2 * (iota(shape, 0) // block_cols) + iota(shape, 1) // width
-        hidden_act = jnp.where(holds_rows(rows, domain_rows), hidden_act.astype(F32), 0.0)
-    hidden_act = hidden_act.astype(BF16)
-
-    fields = [above[:, PAIR:], coarse_ref[:, :PAIR], coarse_ref[:, PAIR:], below[:, :PAIR]]
+    layers = conv_ref.shape[0]
+    cells = [[act[:, half * width : (half + 1) * width] for act in acts] for half in range(2)]
+    for layer in range(layers):
+        parts = shifts(cells, lambda half, at: stage_ref.at[half, at])
+        act = residual_pairs(parts, taps_ref[layer], block_cols).astype(F32)
+        cells = []
+        for half in range(2):
+            runs = []
+            for pair in range(act.shape[0] // block_cols):
+                run = act[pair * block_cols : (pair + 1) * block_cols, half * width : (half + 1) * width]
+                row = 2 * pair + half + layer + 1 - block_rows
+                if not 0 <= row < block_rows:
+                    place = mine * block_rows + row
+                    run = jnp.where(jnp.logical_and(place >= 0, place < domain_rows), run, 0.0)
+                runs.append(run)
+            cells.append(runs)
+
+    above = halo_ref[0].astype(F32)
+    own = coarse_ref[...].astype(F32)
+    below = halo_ref[1].astype(F32)
+    fields = [above[:, PAIR:], own[:, :PAIR], own[:, PAIR:], below[:, :PAIR]]
     lows = [above_low[1]] + own_low + [below_low[0]]
     for pair in range(4):
-        act = hidden_act[pair * block_cols : (pair + 1) * block_cols]
+        act = jnp.concatenate([cells[half][pair] for half in range(2)], axis=1).astype(BF16)
         rest = mxu(head_pair, act, NT)
         wide = 0.0
         for _ in range(3):
             part = rest.astype(BF16)
             wide = wide + mxu(part, spread)
             rest = rest - part.astype(F32)
-        mean = fields[pair].astype(F32) + wide.reshape(channels, PAIR, col_total)
+        mean = fields[pair] + wide.reshape(channels, PAIR, col_total)
         if 1 <= pair <= 2:
             mean_ref[:, (pair - 1) * PAIR : pair * PAIR] = mean
-        low = pool_rows(mean.astype(BF16).astype(F32))
-        low = jnp.concatenate([low, lows[pair]], axis=0)
-        clow_ref[pair] = mxu(narrow, low).astype(BF16)
+        low = pooled(pair_rule, mean.reshape(PAIR * channels, col_total).astype(BF16))
+        clow_ref[pair] = jnp.concatenate([low, lows[pair]], axis=0).astype(BF16)
     for index in range(2, len(moves)):
         finish(index)
-
-
-def holds_rows(rows, domain_rows):
-    return jnp.logical_and(rows >= 0, rows < domain_rows)
 
 
 def edge(coarse, noise, table, lift, conv, head, span):
@@ -256,6 +282,7 @@
         scratch_shapes=[
             pltpu.VMEM((2,) + coarse.shape, BF16),
             pltpu.VMEM((layers, 12 * width, 2 * width), BF16),
+            pltpu.VMEM((2, 3 * strip_rows // PAIR, col_total // POOL + 16, width), F32),
             pltpu.SemaphoreType.DMA((copies,)),
             pltpu.SemaphoreType.DMA((copies,)),
         ],
@@ -338,7 +365,7 @@
 
     lanes = 128
     head_wide = one_hot((channels, lanes), lambda r, c: (c % channels == r) & (c < 4 * feat_rows))
-    head_wide = mxu(head_ref[...], head_wide)
+    head_wide = mxu(head_ref[...], head_wide, TN)
     lane = iota(head_wide.shape, 1)
     heads = []
     for pair in range(2):
@@ -349,7 +376,7 @@
                 heads.append(jnp.where(keep, head_wide, 0.0))
     heads = jnp.concatenate(heads, axis=0).astype(BF16)
 
-    group = stage_ref.shape[1]
+    group = GROUP
     slots = 4 * members
     stage_ref[...] = jnp.zeros_like(stage_ref)
     field_ref[:, slots] = jnp.zeros(field_ref.shape[:1] + field_ref.shape[2:], F32)
@@ -407,26 +434,21 @@
                 sides.append(jnp.concatenate(rows, axis=0))
             parts.append(jnp.concatenate(sides, axis=1).astype(BF16))
         act = residual_pairs(parts, taps_ref[0], stride).astype(F32)
-        parts = [[], [], []]
+        cells = []
         for half in range(2):
-            rows = [[], [], []]
+            runs = []
             for pair in range(3):
                 for at, (offset, _, _) in enumerate(pieces):
                     for member in range(members):
-                        first = ((pair * group + at) * members + member) * block_cols
-                        cells = act[first : first + block_cols, half * width : (half + 1) * width]
+                        first = len(runs) * block_cols
+                        run = act[first : first + block_cols, half * width : (half + 1) * width]
                         if pair == 0 and half == 0:
-                            cells = jnp.where(offset == 0, 0.0, cells)
+                            run = jnp.where(offset == 0, 0.0, run)
                         if pair == 2 and half == 1:
-                            cells = jnp.where(offset == span - 1, 0.0, cells)
-                        hold = stage_ref.at[half, at, pair * members + member]
-                        hold[8 : 8 + block_cols] = cells
-                        rows[0].append(hold[7 : 7 + block_cols])
-                        rows[1].append(cells)
-                        rows[2].append(hold[9 : 9 + block_cols])
-            for tap in range(3):
-                parts[tap].append(jnp.concatenate(rows[tap], axis=0))
-        parts = [jnp.concatenate(sides, axis=1).astype(BF16) for sides in parts]
+                            run = jnp.where(offset == span - 1, 0.0, run)
+                        runs.append(run)
+            cells.append(runs)
+        parts = shifts(cells, lambda half, at: stage_ref.at[half, at])
         act = residual_pairs(parts, taps_ref[1], stride).astype(F32)
         rows = []
         for at in range(group):
@@ -488,7 +510,7 @@
             pltpu.VMEM((weights.shape[0], 3 * 128), F32),
             pltpu.VMEM((strip_rows, feat_rows, col_total), F32),
             pltpu.VMEM((strip_rows, col_total), F32),
-            pltpu.VMEM((2, GROUP, 3 * members, weights.shape[0] // POOL + 16, width), F32),
+            pltpu.VMEM((2, GROUP * 3 * members, weights.shape[0] // POOL + 16, width), F32),
             pltpu.SMEM((weights.shape[0] // strip_rows * slot_total + GROUP,), jnp.int32),
         ],
         name="patches",
@@ -514,9 +536,9 @@
     noise = noise_field.reshape(members * channels, strip_rows, col_total)
     table = jnp.concatenate([anchors, counts[:, None]], axis=1)
     table = jnp.pad(table, ((0, 0), (0, 127 - slot_total)))[None]
-    nlow, clow, mean, tables = edge(coarse, noise, table, regress_lift, regress_conv, regress_head, span)
+    nlow, clow, mean, tables = edge(coarse, noise, table, regress_lift, regress_conv, regress_head.T, span)
     return patches(
-        tables, nlow, clow, mean, noise, blend_weights, denoise_lift, denoise_conv, denoise_head, slot_total
+        tables, nlow, clow, mean, noise, blend_weights, denoise_lift, denoise_conv, denoise_head.T, slot_total
     )
 
 

time: 58.3 us -> 42 us (0.72)
  Pallas kernels: 54.4 us -> 39.2 us
  local copies, waits for them, and re-layouts: 2.05 us -> 1.16 us
    pallas_call x1, Pallas kernels: 37.9 us -> 24.5 us  [patches(): pl.pallas_call(functools.partial(patch_kernel, slot_total), out_shape=(ja...]
    pallas_call x1, Pallas kernels: 16.5 us -> 14.8 us  [edge(): pl.pallas_call(functools.partial(edge_kernel, span), out_shape=(jax.Shape...]
    unnamed x8 -> x2, local copies, waits for them, and re-layouts: 1.53 us -> 0.65 us
where the time goes in v3:
time: 42 us; the launch traced here: 41.8 us
  Pallas kernels  39.2 us (93%)
  between operations  1.29 us (3%)
  local copies, waits for them, and re-layouts  1.16 us (3%)
    pallas_call x1, Pallas kernels, patches(): pl.pallas_call(functools.partial(patch_kernel, slot_total), out_shape=(ja...  24.5 us
    pallas_call x1, Pallas kernels, edge(): pl.pallas_call(functools.partial(edge_kernel, span), out_shape=(jax.Shape...  14.8 us

profile of v3, /device:TPU:25, one launch (start us, length us, event | category | flops | bytes accessed | tf_op | source)
XLA Modules:
  0.0 41.8 jit_solution(1822438377524161762)
XLA Ops:
  1.3 0.0 copy-start
  1.3 0.6 %copy-done = s32[1,2]{1,0:T(1,128)S(1)} copy-done((s32[1,2]{1,0:T(1,128)S(1)}, s32[1,2]{1,0:T(1,128)}, u32[]{:S(2)}) %copy-start) | copy-done | bytes 32
  1.9 0.1 pad_add_fusion
  2.0 0.5 %pad_bitcast_fusion.table_ref = s32[1,1,128]{2,1,0:T(1,128)} fusion(s32[1,3]{1,0:T(1,128)S(1)} %pad_add_fusion), kind=kLoop, calls=%fused_computation.1 | loop fusion | bytes 524 | tf_op jit(solution)/shard_map/broadcast_in_dim | solution.py:538
  2.5 14.8 %edge.1 = (bf16[4,48,512]{2,1,0:T(8,128)(2,1)}, bf16[4,48,512]{2,1,0:T(8,128)(2,1)}, f32[12,16,512]{2,1,0:T(8,128)}, s32[14,1,128]{2,1,0:T(1,128)}) custom-call(bf16[12,16,512]{2,1,0:T(8,128)(2,1)} %coarse_ref.1, bf16[24,16,512]{2,1,0:T(8,128)(2,1)} %bitcast.7, s32[1,1,128]{2,1,0:T(1,128)} %pad_bitcast_fusion.table_ref, bf16[12,128]{1,0:T(8,128)(2,1)} %lift_ref.2, ...), custom_call_target="tpu_custom_call" | custom-call | tf_op jit(solution)/shard_map/edge/pallas_call | solution.py:272
  17.3 24.5 %patches.1 = (f32[12,16,512]{2,1,0:T(8,128)}, f32[12,16,512]{2,1,0:T(8,128)}) custom-call(s32[14,1,128]{2,1,0:T(1,128)} %get-tuple-element.6.table_ref, bf16[4,48,512]{2,1,0:T(8,128)(2,1)} %get-tuple-element.7.nlow_ref, bf16[4,48,512]{2,1,0:T(8,128)(2,1)} %get-tuple-element.8.clow_ref, f32[12,16,512]{2,1,0:T(8,128)} %get-tuple-element.9.mean_ref, ...), custom_call_target="tpu_custom_call" | custom-call | tf_op jit(solution)/shard_map/patches/pallas_call | solution.py:502
Async XLA Ops:
  1.3 0.7 %copy-start = (s32[1,2]{1,0:T(1,128)S(1)}, s32[1,2]{1,0:T(1,128)}, u32[]{:S(2)}) copy-start(s32[1,2]{1,0:T(1,128)} %param.13) | copy-start | bytes 28
